TPU v7x, 32 devices: a whole 2x2x4 slice. The times are simulated.
32 devices in a mesh: px: 8 (over y, x, core), py: 4 (over z).
Axes of the slice: x: 2, y: 2, z: 4, core: 2. Of those that a mesh axis runs over, the one named last changes fastest.
Arguments:
- velocity: float32 [3, 128, 64, 128], P(None, 'px', 'py'), may hold values from -2 to 2
- states: float32 [3, 128, 64, 128], P(None, 'px', 'py'), may hold values from -6 to 6
- solution: float32 [3, 128, 64, 128], P(None, 'px', 'py'), may hold values from -6 to 6
- residual: float32 [3, 128, 64, 128], P(None, 'px', 'py'), may hold values from -6 to 6
- direction: float32 [3, 128, 64, 128], P(None, 'px', 'py'), may hold values from -6 to 6
Outputs:
- new_solution: float32 [3, 128, 64, 128], P(None, 'px', 'py')
- new_residual: float32 [3, 128, 64, 128], P(None, 'px', 'py')
- new_direction: float32 [3, 128, 64, 128], P(None, 'px', 'py')
All inputs are finite; a program needn't handle non-finite values.
Results may differ from a plain program's by a relative error of at most 0.0001.
Values sent between devices are 32-bit elements; how exact they have to be, the bound alone decides.
A program may use at most 64 MiB of HBM per device.

v0:
```python
import functools

import jax
import jax.numpy as jnp
from jax import lax
from jax.experimental import pallas as pl
from jax.experimental.pallas import tpu as pltpu
from jax.sharding import PartitionSpec as P

W = 4
DIRS = ((1, 0), (-1, 0), (0, 1), (0, -1), (1, 1), (1, -1), (-1, 1), (-1, -1))
HI = lax.Precision.HIGHEST
WEIGHT = 0.8 / 0.65


def up(v, axis):
    return pltpu.roll(v, v.shape[axis] - 1, axis)


def down(v, axis):
    return pltpu.roll(v, 1, axis)


def kernel(
    px, py, vel, sta, res, dirn, o_img, o_pr, o_sc,
    F, FV, RS, S, T, U, G, IMG, TR, CB, PR, AR,
    loc_sem, h_send, h_recv, s_send, s_recv, u_send, u_recv, c_send, c_recv, a_send, a_recv, out_sem,
):
    nx, ny, nz = sta.shape[1:]
    ex, ey = nx + 2 * W, ny + 2 * W
    me_x, me_y = lax.axis_index("px"), lax.axis_index("py")

    def at(dx, dy):
        return (lax.rem(me_x + (dx + px), px), lax.rem(me_y + (dy + py), py))

    def mesh_copy(src, dst, s, r, dx, dy):
        return pltpu.make_async_remote_copy(
            src_ref=src, dst_ref=dst, send_sem=s, recv_sem=r,
            device_id=at(dx, dy), device_id_type=pl.DeviceIdType.MESH,
        )

    locals_ = []
    for g, a in enumerate((sta, dirn, vel)):
        locals_.append(
            pltpu.make_async_copy(a, F.at[pl.ds(3 * g, 3), pl.ds(W, nx), pl.ds(0, ny)], loc_sem.at[g])
        )
    locals_.append(pltpu.make_async_copy(res, RS, loc_sem.at[3]))

    barrier = pltpu.get_barrier_semaphore()
    total = px * py

    def peer(d):
        other = lax.rem(me_x * py + me_y + d, total)
        return (other // py, lax.rem(other, py))

    def each_peer(body):
        def run(i, carry):
            body(i + 1)
            return carry

        lax.fori_loop(0, total - 1, run, 0, unroll=total <= 64)

    each_peer(
        lambda d: pl.semaphore_signal(
            barrier, inc=1, device_id=peer(d), device_id_type=pl.DeviceIdType.MESH
        )
    )
    for c in locals_:
        c.start()
    pl.semaphore_wait(barrier, total - 1)

    def x_span(dx, w, k):
        return {
            0: (0, nx, W),
            1: (nx - w - k, w, W - w - k),
            -1: (k, w, W + nx + k),
        }[dx]

    def y_span(dy, w, k):
        return {
            0: (0, ny, 0),
            1: (ny - w - k, w, ny + 2 * W - w - k),
            -1: (k, w, ny + k),
        }[dy]

    def halo(make, send, recv, width, corner, base=0):
        copies = []
        for i, (dx, dy) in enumerate(DIRS):
            if dx and dy:
                if not corner:
                    continue
                wide = (corner, corner)
                start = (0, 0)
            else:
                wide = (width, width)
                start = (base, base)
            sx, lx, tx = x_span(dx, wide[0], start[0])
            sy, ly, ty = y_span(dy, wide[1], start[1])
            src, dst = make((pl.ds(sx, lx), pl.ds(sy, ly)), (pl.ds(tx, lx), pl.ds(ty, ly)))
            copies.append(mesh_copy(src, dst, send.at[i], recv.at[i], dx, dy))
        for c in copies:
            c.start()
        return copies

    def field_halo(g, a, slot, *args):
        return halo(
            lambda src, dst: (a.at[(pl.ds(0, 3),) + src], F.at[(pl.ds(3 * g, 3),) + dst]),
            h_send.at[slot], h_recv.at[slot], *args,
        )

    state_copies = field_halo(0, sta, 0, 1, 0)
    near_copies = field_halo(2, vel, 1, 2, 3)

    row = lambda shape: lax.broadcasted_iota(jnp.int32, shape, 0)
    lane = lambda shape: lax.broadcasted_iota(jnp.int32, shape, 1)
    cz = nz // 4
    cx, cy = nx // 4, ny // 4
    lanes = cy * cz
    n_rows = 6 * cx * ny
    m_shape = (nz, lanes)
    gather_z = (row(m_shape) // 4 == lax.rem(lane(m_shape), cz)).astype(jnp.float32)
    t_shape = (lanes, nz)
    spread_z = (lax.rem(row(t_shape), cz) == lane(t_shape) // 4).astype(jnp.float32)
    k_shape = (n_rows, lanes)
    keep = lax.rem(row(k_shape), ny) // 4 == lane(k_shape) // cz
    r_shape = (cx * 8, n_rows)
    src_c, src_x = lane(r_shape) // (cx * ny), lax.rem(lane(r_shape) // ny, cx)
    gather_y = jnp.where(
        jnp.logical_and(row(r_shape) // 8 == src_x, lax.rem(row(r_shape), 8) == src_c), 1.0 / 64.0, 0.0
    )
    p_shape = (n_rows, cx * 8)
    dst_c, dst_x = row(p_shape) // (cx * ny), lax.rem(row(p_shape) // ny, cx)
    spread_y = jnp.where(
        jnp.logical_and(lane(p_shape) // 8 == dst_x, lax.rem(lane(p_shape), 8) == dst_c), 1.0, 0.0
    )

    def sweep(start, planes, step, body):
        def run(i, carry):
            body(start + i * step)
            return carry

        lax.fori_loop(0, planes // step, run, 0, unroll=True)

    for c in locals_[:2]:
        c.wait()
    for c in state_copies:
        c.wait()

    def sources(x):
        own = pl.ds(x, 2)
        at_x = pl.ds(x - W, 2)
        d = [F[3 + k, own, pl.ds(0, ny)] for k in range(3)]
        for n in range(3):
            f = F[n, own]
            grads = (
                (F[n, pl.ds(x + 1, 2)] - F[n, pl.ds(x - 1, 2)])[:, :ny],
                (up(f, 1) - down(f, 1))[:, :ny],
                (up(f, 2) - down(f, 2))[:, :ny],
            )
            S[n, own, pl.ds(0, ny)] = 0.5 * (d[0] * grads[0] + d[1] * grads[1] + d[2] * grads[2])
            for k in range(3):
                G[3 * n + k, at_x] = grads[k]

    sweep(W, nx, 2, sources)
    source_copies = halo(
        lambda src, dst: (
            S.at[pl.ds(0, 2), pl.ds(W + src[0].start, src[0].size), src[1]],
            S.at[(pl.ds(0, 2),) + dst],
        ),
        s_send, s_recv, 3, 2,
    )
    far_copies = halo(
        lambda src, dst: (
            vel.at[(pl.ds(0, 3),) + src],
            FV.at[pl.ds(0, 3), pl.ds(0, nx), pl.ds(dst[1].start - ny, 2)]
            if dst[1].size == 2
            else F.at[(pl.ds(6, 3),) + dst],
        ),
        h_send.at[2], h_recv.at[2], 2, 0, 2,
    )
    direction_copies = field_halo(1, dirn, 3, 1, 0)

    locals_[3].wait()
    rr = jnp.zeros((ny, nz), jnp.float32)
    for c in range(3):
        for b in range(cx):
            r = RS[c, pl.ds(4 * b, 4)]
            TR[c, b] = jnp.sum(r, axis=0)
            rr = rr + jnp.sum(r * r, axis=0)

    locals_[2].wait()
    for c in near_copies:
        c.wait()
    for c in source_copies:
        c.wait()

    def advect(read, x):
        f = read(x)
        v = [F[6 + k, pl.ds(x, 2)] for k in range(3)]
        return f, 0.5 * (
            v[0] * (read(x + 1) - read(x - 1))
            + v[1] * (up(f, 1) - down(f, 1))
            + v[2] * (up(f, 2) - down(f, 2))
        )

    def forward_one(x):
        f, adv = advect(lambda i: S[0, pl.ds(i, 2)], x)
        at_x = pl.ds(x, 2)
        T[1, at_x] = 0.25 * (0.5 * adv - S[1, at_x] - f)

    def forward_two(x):
        f, adv = advect(lambda i: T[1, pl.ds(i, 2)], x)
        at_x = pl.ds(x, 2)
        first = -(adv + S[1, at_x])
        T[2, at_x] = f + 0.5 * first
        T[3, at_x] = f + 0.25 * first

    def forward_three(x):
        f, adv = advect(lambda i: T[2, pl.ds(i, 2)], x)
        at_x = pl.ds(x, 2)
        U[at_x, pl.ds(0, ny)] = 0.25 * (adv[:, :ny] + S[2, at_x, pl.ds(0, ny)]) - T[3, at_x, pl.ds(0, ny)]

    sweep(2, ex - 4, 2, forward_one)
    sweep(3, ex - 6, 2, forward_two)
    sweep(4, ex - 8, 2, forward_three)

    u_copies = halo(
        lambda src, dst: (U.at[pl.ds(W + src[0].start, src[0].size), src[1]], U.at[dst]),
        u_send, u_recv, W, 3,
    )
    for c in direction_copies:
        c.wait()

    def base(x):
        own = pl.ds(x, 2)
        at_x = pl.ds(x - W, 2)
        adj = 0.125 * U[own, pl.ds(0, ny)]
        for k in range(3):
            f = F[3 + k, own]
            neighbours = (
                F[3 + k, pl.ds(x + 1, 2)] + F[3 + k, pl.ds(x - 1, 2)]
                + up(f, 1) + down(f, 1) + up(f, 2) + down(f, 2)
            )[:, :ny]
            IMG[k, at_x] = 4.0 * f[:, :ny] - 0.5 * neighbours + adj * G[6 + k, at_x]

    sweep(W, nx, 2, base)
    for c in far_copies:
        c.wait()
    tile_row = lax.broadcasted_iota(jnp.int32, (1, 1, 2 * W, nz), 2)
    band, beyond = pl.ds(W, nx), pl.ds(ny, 2 * W)
    from_far = jnp.logical_and(tile_row >= 2, tile_row < 2 * W - 2)
    F[pl.ds(6, 3), band, beyond] = jnp.where(from_far, FV[...], F[pl.ds(6, 3), band, beyond])
    for c in u_copies:
        c.wait()

    def diverge(read, x):
        f = read(x)
        flux_y = f * F[7, pl.ds(x, 2)]
        flux_z = f * F[8, pl.ds(x, 2)]
        return f, 0.5 * (
            read(x + 1) * F[6, pl.ds(x + 1, 2)]
            - read(x - 1) * F[6, pl.ds(x - 1, 2)]
            + (up(flux_y, 1) - down(flux_y, 1))
            + (up(flux_z, 2) - down(flux_z, 2))
        )

    def adjoint_first(read):
        def body(x):
            f, rate = diverge(read, x)
            at_x = pl.ds(x, 2)
            T[0, at_x] = f + 0.5 * rate
            T[1, at_x] = f + 0.25 * rate

        return body

    def adjoint_second(x):
        f, rate = diverge(lambda i: T[0, pl.ds(i, 2)], x)
        at_x = pl.ds(x, 2)
        T[2, at_x] = T[1, at_x] + 0.25 * rate

    def adjoint_last(x):
        f, rate = diverge(lambda i: T[0, pl.ds(i, 2)], x)
        own = pl.ds(x, 2)
        at_x = pl.ds(x - W, 2)
        adj_zero = 0.125 * (T[1, own] + 0.25 * rate)[:, :ny]
        adj_one = 0.25 * T[2, own, pl.ds(0, ny)]
        for k in range(3):
            IMG[k, at_x] = IMG[k, at_x] + adj_one * G[3 + k, at_x] + adj_zero * G[k, at_x]

    sweep(1, ex - 2, 2, adjoint_first(lambda i: U[pl.ds(i, 2)]))
    sweep(2, ex - 4, 2, adjoint_second)
    sweep(3, ex - 6, 2, adjoint_first(lambda i: T[2, pl.ds(i, 2)]))
    sweep(4, ex - 8, 2, adjoint_last)

    image_out = pltpu.make_async_copy(IMG, o_img, out_sem.at[0])
    image_out.start()
    for c in range(3):
        for b in range(cx):
            TR[3 + c, b] = jnp.sum(IMG[c, pl.ds(4 * b, 4)], axis=0)
    z_sums = jnp.dot(TR[...].reshape(n_rows, nz), gather_z, precision=HI, preferred_element_type=jnp.float32)
    rhs = jnp.dot(
        gather_y, jnp.where(keep, z_sums, 0.0), precision=HI, preferred_element_type=jnp.float32
    )
    CB[1, 1] = rhs.reshape(cx, 8, lanes)

    c_copies = []
    for i, (dx, dy) in enumerate(DIRS):
        c = mesh_copy(CB.at[1, 1], CB.at[1 - dx, 1 - dy], c_send.at[i], c_recv.at[i], dx, dy)
        c.start()
        c_copies.append(c)

    rq = jnp.zeros((ny, nz), jnp.float32)
    qq = jnp.zeros((ny, nz), jnp.float32)
    dq = jnp.zeros((ny, nz), jnp.float32)
    for c in range(3):
        for b in range(cx):
            q = IMG[c, pl.ds(4 * b, 4)]
            rq = rq + jnp.sum(q * RS[c, pl.ds(4 * b, 4)], axis=0)
            qq = qq + jnp.sum(q * q, axis=0)
            dq = dq + jnp.sum(q * F[3 + c, pl.ds(W + 4 * b, 4)][:, :ny], axis=0)
    flat = lambda v: jnp.sum(v, axis=0, keepdims=True)
    rr, rq, qq, dq = flat(rr), flat(rq), flat(qq), flat(dq)

    for c in c_copies:
        c.wait()
    b_all = jnp.concatenate(
        [jnp.concatenate([CB[a, e] for e in range(3)], axis=2) for a in range(3)], axis=0
    )
    b_all = b_all[cx - 3 : 2 * cx + 3]
    z_pos = lax.rem(lax.broadcasted_iota(jnp.int32, (1, 8, 3 * lanes), 2), cz)
    total_lanes = 3 * lanes
    approx = WEIGHT * b_all
    for turn in range(3):
        mid = approx[1:-1]
        z_up = jnp.where(z_pos == cz - 1, pltpu.roll(mid, cz - 1, 2), pltpu.roll(mid, total_lanes - 1, 2))
        z_down = jnp.where(z_pos == 0, pltpu.roll(mid, total_lanes - cz + 1, 2), pltpu.roll(mid, 1, 2))
        around = (
            approx[2:] + approx[:-2]
            + pltpu.roll(mid, cz, 2) + pltpu.roll(mid, total_lanes - cz, 2)
            + z_up + z_down
        )
        approx = 0.2 * mid + WEIGHT * (b_all[turn + 1 : -turn - 1] + 0.1 * around)
    e = approx[:, :, lanes : 2 * lanes]
    b_own = CB[1, 1]
    same = jnp.sum(b_own * e, axis=0)
    r8 = row((8, lanes))
    cross = jnp.sum(b_own * jnp.where(r8[None] < 3, pltpu.roll(e, 5, 1), pltpu.roll(e, 3, 1)), axis=0)
    pick = lambda v, lo, hi: flat(jnp.where(jnp.logical_and(r8 >= lo, r8 < hi), v, 0.0))
    sum_a = 0.25 * rr + 64.0 * pick(same, 0, 3)
    sum_b = 0.5 * rq + 64.0 * pick(cross, 0, 6)
    sum_c = 0.25 * qq + 64.0 * pick(same, 3, 6)
    whole = lambda v: jnp.broadcast_to(jnp.sum(v, axis=1, keepdims=True), (1, lanes))
    l1 = lane((1, lanes))
    AR[0] = jnp.where(
        l1 == 0, whole(sum_a), jnp.where(l1 == 1, whole(sum_b), jnp.where(l1 == 2, whole(sum_c), whole(dq)))
    )

    def sums_copy(d):
        other = peer(d)
        return pltpu.make_async_remote_copy(
            src_ref=AR.at[0], dst_ref=AR.at[d], send_sem=a_send.at[d], recv_sem=a_recv.at[d],
            device_id=other, device_id_type=pl.DeviceIdType.MESH,
        )

    each_peer(lambda d: sums_copy(d).start())

    spread = jnp.dot(spread_y, e.reshape(cx * 8, lanes), precision=HI, preferred_element_type=jnp.float32)
    fine = jnp.dot(jnp.where(keep, spread, 0.0), spread_z, precision=HI, preferred_element_type=jnp.float32)
    PR[...] = fine.reshape(6, cx, ny, nz)

    coarse_out = pltpu.make_async_copy(PR, o_pr, out_sem.at[1])
    coarse_out.start()
    each_peer(lambda d: sums_copy(d).wait())
    sums = jnp.sum(AR[...], axis=0)
    rz, mixed, square, curvature = (
        jnp.sum(jnp.where(l1 == i, sums, 0.0), axis=1, keepdims=True) for i in range(4)
    )
    alpha = rz / curvature
    beta = (rz - alpha * mixed + alpha * alpha * square) / rz
    o_sc[...] = jnp.where(r8 == 0, alpha, beta)
    image_out.wait()
    coarse_out.wait()


def finish(scalars, res_coarse, img_coarse, image, sol, res, dirn, o_sol, o_res, o_dir):
    alpha, beta = scalars[0:1, 0:1].reshape(1, 1, 1), scalars[1:2, 0:1].reshape(1, 1, 1)
    for b in range(res_coarse.shape[1]):
        at_x = pl.ds(4 * b, 4)
        d = dirn[0, at_x]
        left = res[0, at_x] - alpha * image[0, at_x]
        coarse = res_coarse[0, pl.ds(b, 1)] - alpha * img_coarse[0, pl.ds(b, 1)]
        o_sol[0, at_x] = sol[0, at_x] + alpha * d
        o_res[0, at_x] = left
        o_dir[0, at_x] = 0.25 * left + coarse + beta * d


def solution(mesh):
    px, py = mesh.shape["px"], mesh.shape["py"]
    spec = P(None, "px", "py", None)

    def local(velocity, states, solution, residual, direction):
        comps, nx, ny, nz = velocity.shape
        ex, ey = nx + 2 * W, ny + 2 * W
        cx = nx // 4
        lanes = (ny // 4) * (nz // 4)
        f32 = jnp.float32
        dma = pltpu.SemaphoreType.DMA
        shape = jax.ShapeDtypeStruct
        anywhere = pl.BlockSpec(memory_space=pl.ANY)
        image, spread, scalars = pl.pallas_call(
                functools.partial(kernel, px, py),
                out_shape=[shape(velocity.shape, f32), shape((6, cx, ny, nz), f32), shape((8, lanes), f32)],
                in_specs=[anywhere] * 4,
                out_specs=[anywhere, anywhere, pl.BlockSpec(memory_space=pltpu.VMEM)],
                scratch_shapes=[
                    pltpu.VMEM((9, ex, ey, nz), f32),
                    pltpu.VMEM((3, nx, 2 * W, nz), f32),
                    pltpu.VMEM((3, nx, ny, nz), f32),
                    pltpu.VMEM((3, ex, ey, nz), f32),
                    pltpu.VMEM((4, ex, ey, nz), f32),
                    pltpu.VMEM((ex, ey, nz), f32),
                    pltpu.VMEM((9, nx, ny, nz), f32),
                    pltpu.VMEM((3, nx, ny, nz), f32),
                    pltpu.VMEM((6, cx, ny, nz), f32),
                    pltpu.VMEM((3, 3, cx, 8, lanes), f32),
                    pltpu.VMEM((6, cx, ny, nz), f32),
                    pltpu.VMEM((px * py, 1, lanes), f32),
                    dma((4,)),
                    dma((4, 8)),
                    dma((4, 8)),
                    dma((8,)),
                    dma((8,)),
                    dma((8,)),
                    dma((8,)),
                    dma((8,)),
                    dma((8,)),
                    dma((px * py,)),
                    dma((px * py,)),
                    dma((2,)),
                ],
                compiler_params=pltpu.CompilerParams(
                    collective_id=0, has_side_effects=True
                ),
            )(velocity, states, residual, direction)
        part = pl.BlockSpec((1, nx, ny, nz), lambda c: (c, 0, 0, 0))
        return tuple(
            pl.pallas_call(
                finish,
                grid=(3,),
                out_shape=[shape(velocity.shape, f32)] * 3,
                in_specs=[
                    pl.BlockSpec((8, lanes), lambda c: (0, 0)),
                    pl.BlockSpec((1, cx, ny, nz), lambda c: (c, 0, 0, 0)),
                    pl.BlockSpec((1, cx, ny, nz), lambda c: (c + 3, 0, 0, 0)),
                    part, part, part, part,
                ],
                out_specs=[part] * 3,
            )(scalars, spread, spread, image, solution, residual, direction)
        )

    return jax.shard_map(local, mesh=mesh, in_specs=(spec,) * 5, out_specs=(spec,) * 3, check_vma=False)
```

profile of v0, /device:TPU:0, one launch (start us, length us, event | category | flops | bytes accessed | tf_op | source)
XLA Modules:
  0.0 40.9 jit_solution(11650736941950728081)
XLA Ops:
  0.6 36.8 %shard_map.76 = (f32[3,16,16,128]{3,2,1,0:T(8,128)}, f32[6,4,16,128]{3,2,1,0:T(8,128)}, f32[8,128]{1,0:T(8,128)}) custom-call(f32[3,16,16,128]{3,2,1,0:T(8,128)} %vel.1, f32[3,16,16,128]{3,2,1,0:T(8,128)} %sta.1, f32[3,16,16,128]{3,2,1,0:T(8,128)} %res.3, f32[3,16,16,128]{3,2,1,0:T(8,128)} %dirn.3), custom_call_target="tpu_custom_call" | custom-call | tf_op jit(solution)/shard_map/pallas_call | solution.py:410
  37.5 3.4 %shard_map.77 = (f32[3,16,16,128]{3,2,1,0:T(8,128)}, f32[3,16,16,128]{3,2,1,0:T(8,128)}, f32[3,16,16,128]{3,2,1,0:T(8,128)}) custom-call(f32[8,128]{1,0:T(8,128)} %get-tuple-element.6.scalars, f32[6,4,16,128]{3,2,1,0:T(8,128)} %get-tuple-element.7.res_coarse.img_coarse, f32[6,4,16,128]{3,2,1,0:T(8,128)} %get-tuple-element.7.res_coarse.img_coarse, ...), custom_call_target="tpu_custom_call" | custom-call | tf_op jit(solution)/shard_map/pallas_call | solution.py:447
where the time goes:
time: 41 us; the launch traced here: 40.9 us
  Pallas kernels  40.2 us (98%)
  between operations  0.64 us (2%)
    pallas_call x1, Pallas kernels, local(): pl.pallas_call(functools.partial(kernel, px, py), out_shape=[shape(veloci...  36.8 us
    pallas_call x1, Pallas kernels, local(): pl.pallas_call(finish, grid=(3,), out_shape=[shape(velocity.shape, f32)]...  3.41 us

commit v1 on v0

--- a/solution.py
+++ b/solution.py
@@ -22,9 +22,9 @@
 
 
 def kernel(
-    px, py, vel, sta, res, dirn, o_img, o_pr, o_sc,
-    F, FV, RS, S, T, U, G, IMG, TR, CB, PR, AR,
-    loc_sem, h_send, h_recv, s_send, s_recv, u_send, u_recv, c_send, c_recv, a_send, a_recv, out_sem,
+    px, py, vel, sta, sol, res, dirn, IMG, PR, o_sc, KEEP,
+    F, FV, S, T, U, G, TR, CB, AR,
+    loc_sem, h_send, h_recv, s_send, s_recv, u_send, u_recv, c_send, c_recv, a_send, a_recv,
 ):
     nx, ny, nz = sta.shape[1:]
     ex, ey = nx + 2 * W, ny + 2 * W
@@ -44,7 +44,9 @@
         locals_.append(
             pltpu.make_async_copy(a, F.at[pl.ds(3 * g, 3), pl.ds(W, nx), pl.ds(0, ny)], loc_sem.at[g])
         )
-    locals_.append(pltpu.make_async_copy(res, RS, loc_sem.at[3]))
+    for i, a in enumerate((res, dirn, sol)):
+        locals_.append(pltpu.make_async_copy(a, KEEP.at[i], loc_sem.at[3 + i]))
+    RS = KEEP.at[0]
 
     barrier = pltpu.get_barrier_semaphore()
     total = px * py
@@ -292,8 +294,6 @@
     sweep(3, ex - 6, 2, adjoint_first(lambda i: T[2, pl.ds(i, 2)]))
     sweep(4, ex - 8, 2, adjoint_last)
 
-    image_out = pltpu.make_async_copy(IMG, o_img, out_sem.at[0])
-    image_out.start()
     for c in range(3):
         for b in range(cx):
             TR[3 + c, b] = jnp.sum(IMG[c, pl.ds(4 * b, 4)], axis=0)
@@ -368,8 +368,6 @@
     fine = jnp.dot(jnp.where(keep, spread, 0.0), spread_z, precision=HI, preferred_element_type=jnp.float32)
     PR[...] = fine.reshape(6, cx, ny, nz)
 
-    coarse_out = pltpu.make_async_copy(PR, o_pr, out_sem.at[1])
-    coarse_out.start()
     each_peer(lambda d: sums_copy(d).wait())
     sums = jnp.sum(AR[...], axis=0)
     rz, mixed, square, curvature = (
@@ -378,20 +376,28 @@
     alpha = rz / curvature
     beta = (rz - alpha * mixed + alpha * alpha * square) / rz
     o_sc[...] = jnp.where(r8 == 0, alpha, beta)
-    image_out.wait()
-    coarse_out.wait()
-
-
-def finish(scalars, res_coarse, img_coarse, image, sol, res, dirn, o_sol, o_res, o_dir):
+    for c in locals_[4:]:
+        c.wait()
+
+
+def finish(scalars, coarse, image, keep, o_sol, o_res, o_dir, N, sem):
     alpha, beta = scalars[0:1, 0:1].reshape(1, 1, 1), scalars[1:2, 0:1].reshape(1, 1, 1)
-    for b in range(res_coarse.shape[1]):
-        at_x = pl.ds(4 * b, 4)
-        d = dirn[0, at_x]
-        left = res[0, at_x] - alpha * image[0, at_x]
-        coarse = res_coarse[0, pl.ds(b, 1)] - alpha * img_coarse[0, pl.ds(b, 1)]
-        o_sol[0, at_x] = sol[0, at_x] + alpha * d
-        o_res[0, at_x] = left
-        o_dir[0, at_x] = 0.25 * left + coarse + beta * d
+    copies = []
+    for c in range(3):
+        for b in range(coarse.shape[1]):
+            at_x = pl.ds(4 * b, 4)
+            d = keep[1, c, at_x]
+            left = keep[0, c, at_x] - alpha * image[c, at_x]
+            mixed = coarse[c, pl.ds(b, 1)] - alpha * coarse[3 + c, pl.ds(b, 1)]
+            N[0, c, at_x] = keep[2, c, at_x] + alpha * d
+            N[1, c, at_x] = left
+            N[2, c, at_x] = 0.25 * left + mixed + beta * d
+        for i, out in enumerate((o_sol, o_res, o_dir)):
+            copy = pltpu.make_async_copy(N.at[i, c], out.at[c], sem.at[3 * i + c])
+            copy.start()
+            copies.append(copy)
+    for copy in copies:
+        copy.wait()
 
 
 def solution(mesh):
@@ -407,25 +413,26 @@
         dma = pltpu.SemaphoreType.DMA
         shape = jax.ShapeDtypeStruct
         anywhere = pl.BlockSpec(memory_space=pl.ANY)
-        image, spread, scalars = pl.pallas_call(
+        vmem = pl.BlockSpec(memory_space=pltpu.VMEM)
+        image, spread, scalars, keep = pl.pallas_call(
                 functools.partial(kernel, px, py),
-                out_shape=[shape(velocity.shape, f32), shape((6, cx, ny, nz), f32), shape((8, lanes), f32)],
-                in_specs=[anywhere] * 4,
-                out_specs=[anywhere, anywhere, pl.BlockSpec(memory_space=pltpu.VMEM)],
+                out_shape=[
+                    shape(velocity.shape, f32), shape((6, cx, ny, nz), f32), shape((8, lanes), f32),
+                    shape((3,) + velocity.shape, f32),
+                ],
+                in_specs=[anywhere] * 5,
+                out_specs=[vmem] * 4,
                 scratch_shapes=[
                     pltpu.VMEM((9, ex, ey, nz), f32),
                     pltpu.VMEM((3, nx, 2 * W, nz), f32),
-                    pltpu.VMEM((3, nx, ny, nz), f32),
                     pltpu.VMEM((3, ex, ey, nz), f32),
                     pltpu.VMEM((4, ex, ey, nz), f32),
                     pltpu.VMEM((ex, ey, nz), f32),
                     pltpu.VMEM((9, nx, ny, nz), f32),
-                    pltpu.VMEM((3, nx, ny, nz), f32),
                     pltpu.VMEM((6, cx, ny, nz), f32),
                     pltpu.VMEM((3, 3, cx, 8, lanes), f32),
-                    pltpu.VMEM((6, cx, ny, nz), f32),
                     pltpu.VMEM((px * py, 1, lanes), f32),
-                    dma((4,)),
+                    dma((6,)),
                     dma((4, 8)),
                     dma((4, 8)),
                     dma((8,)),
@@ -436,26 +443,20 @@
                     dma((8,)),
                     dma((px * py,)),
                     dma((px * py,)),
-                    dma((2,)),
                 ],
                 compiler_params=pltpu.CompilerParams(
-                    collective_id=0, has_side_effects=True
+                    collective_id=0, has_side_effects=True, vmem_limit_bytes=24 * 2**20
                 ),
-            )(velocity, states, residual, direction)
-        part = pl.BlockSpec((1, nx, ny, nz), lambda c: (c, 0, 0, 0))
+            )(*(pltpu.with_memory_space_constraint(a, pltpu.HBM) for a in (velocity, states, solution, residual, direction)))
         return tuple(
             pl.pallas_call(
                 finish,
-                grid=(3,),
                 out_shape=[shape(velocity.shape, f32)] * 3,
-                in_specs=[
-                    pl.BlockSpec((8, lanes), lambda c: (0, 0)),
-                    pl.BlockSpec((1, cx, ny, nz), lambda c: (c, 0, 0, 0)),
-                    pl.BlockSpec((1, cx, ny, nz), lambda c: (c + 3, 0, 0, 0)),
-                    part, part, part, part,
-                ],
-                out_specs=[part] * 3,
-            )(scalars, spread, spread, image, solution, residual, direction)
+                in_specs=[vmem] * 4,
+                out_specs=[anywhere] * 3,
+                scratch_shapes=[pltpu.VMEM((3,) + velocity.shape, f32), dma((9,))],
+                compiler_params=pltpu.CompilerParams(vmem_limit_bytes=8 * 2**20),
+            )(scalars, spread, image, keep)
         )
 
     return jax.shard_map(local, mesh=mesh, in_specs=(spec,) * 5, out_specs=(spec,) * 3, check_vma=False)

time: 41 us -> 38.2 us (0.932)
  Pallas kernels: 40.2 us -> 37.4 us
    pallas_call x1, Pallas kernels: 3.41 us -> 1.16 us  [local(): pl.pallas_call(finish, out_shape=[shape(velocity.shape, f32)] * 3, in_spe...]
    pallas_call x1, Pallas kernels: 36.8 us -> 36.2 us  [local(): pl.pallas_call(functools.partial(kernel, px, py), out_shape=[shape(veloci...]
where the time goes in v1:
time: 38.2 us; the launch traced here: 38 us
  Pallas kernels  37.4 us (98%)
  between operations  0.64 us (2%)
    pallas_call x1, Pallas kernels, local(): pl.pallas_call(functools.partial(kernel, px, py), out_shape=[shape(veloci...  36.2 us
    pallas_call x1, Pallas kernels, local(): pl.pallas_call(finish, out_shape=[shape(velocity.shape, f32)] * 3, in_spe...  1.16 us

profile of v1, /device:TPU:0, one launch (start us, length us, event | category | flops | bytes accessed | tf_op | source)
XLA Modules:
  0.0 38.0 jit_solution(12619627099369160551)
XLA Ops:
  0.6 36.2 %shard_map.76 = (f32[3,16,16,128]{3,2,1,0:T(8,128)S(1)}, f32[6,4,16,128]{3,2,1,0:T(8,128)S(1)}, f32[8,128]{1,0:T(8,128)S(1)}, f32[3,3,16,16,128]{4,3,2,1,0:T(8,128)S(1)}) custom-call(f32[3,16,16,128]{3,2,1,0:T(8,128)} %vel.1, f32[3,16,16,128]{3,2,1,0:T(8,128)} %sta.1, f32[3,16,16,128]{3,2,1,0:T(8,128)} %sol.1, f32[3,16,16,128]{3,2,1,0:T(8,128)} %res.1, ...), custom_call_target="tpu_custom_call" | custom-call | tf_op jit(solution)/shard_map/pallas_call | solution.py:417
  36.9 1.2 %shard_map.77 = (f32[3,16,16,128]{3,2,1,0:T(8,128)}, f32[3,16,16,128]{3,2,1,0:T(8,128)}, f32[3,16,16,128]{3,2,1,0:T(8,128)}) custom-call(f32[8,128]{1,0:T(8,128)S(1)} %get-tuple-element.7.scalars, f32[6,4,16,128]{3,2,1,0:T(8,128)S(1)} %get-tuple-element.8.coarse, f32[3,16,16,128]{3,2,1,0:T(8,128)S(1)} %get-tuple-element.9.image, ...), custom_call_target="tpu_custom_call" | custom-call | tf_op jit(solution)/shard_map/pallas_call | solution.py:452

commit v2 on v1

--- a/solution.py
+++ b/solution.py
@@ -8,7 +8,9 @@
 from jax.sharding import PartitionSpec as P
 
 W = 4
-DIRS = ((1, 0), (-1, 0), (0, 1), (0, -1), (1, 1), (1, -1), (-1, 1), (-1, -1))
+SIDES = ((0, 1), (0, -1), (1, 0), (-1, 0))
+CORNERS = ((1, 1), (1, -1), (-1, 1), (-1, -1))
+DIRS = SIDES + CORNERS
 HI = lax.Precision.HIGHEST
 WEIGHT = 0.8 / 0.65
 
@@ -23,7 +25,7 @@
 
 def kernel(
     px, py, vel, sta, sol, res, dirn, IMG, PR, o_sc, KEEP,
-    F, FV, S, T, U, G, TR, CB, AR,
+    F, FV, FC, S, T, U, G, CB, AR,
     loc_sem, h_send, h_recv, s_send, s_recv, u_send, u_recv, c_send, c_recv, a_send, a_recv,
 ):
     nx, ny, nz = sta.shape[1:]
@@ -62,14 +64,19 @@
 
         lax.fori_loop(0, total - 1, run, 0, unroll=total <= 64)
 
-    each_peer(
-        lambda d: pl.semaphore_signal(
-            barrier, inc=1, device_id=peer(d), device_id_type=pl.DeviceIdType.MESH
-        )
-    )
+    small = max(px // 2 - 3, 0) + max(py // 2 - 3, 0) <= 2
+    if small:
+        for dx, dy in SIDES:
+            pl.semaphore_signal(barrier, inc=1, device_id=at(dx, dy), device_id_type=pl.DeviceIdType.MESH)
+    else:
+        each_peer(
+            lambda d: pl.semaphore_signal(
+                barrier, inc=1, device_id=peer(d), device_id_type=pl.DeviceIdType.MESH
+            )
+        )
     for c in locals_:
         c.start()
-    pl.semaphore_wait(barrier, total - 1)
+    pl.semaphore_wait(barrier, len(SIDES) if small else total - 1)
 
     def x_span(dx, w, k):
         return {
@@ -85,19 +92,11 @@
             -1: (k, w, ny + k),
         }[dy]
 
-    def halo(make, send, recv, width, corner, base=0):
+    def halo(make, send, recv, dirs, width, base=0):
         copies = []
-        for i, (dx, dy) in enumerate(DIRS):
-            if dx and dy:
-                if not corner:
-                    continue
-                wide = (corner, corner)
-                start = (0, 0)
-            else:
-                wide = (width, width)
-                start = (base, base)
-            sx, lx, tx = x_span(dx, wide[0], start[0])
-            sy, ly, ty = y_span(dy, wide[1], start[1])
+        for i, (dx, dy) in enumerate(dirs):
+            sx, lx, tx = x_span(dx, width, base)
+            sy, ly, ty = y_span(dy, width, base)
             src, dst = make((pl.ds(sx, lx), pl.ds(sy, ly)), (pl.ds(tx, lx), pl.ds(ty, ly)))
             copies.append(mesh_copy(src, dst, send.at[i], recv.at[i], dx, dy))
         for c in copies:
@@ -110,8 +109,8 @@
             h_send.at[slot], h_recv.at[slot], *args,
         )
 
-    state_copies = field_halo(0, sta, 0, 1, 0)
-    near_copies = field_halo(2, vel, 1, 2, 3)
+    state_copies = field_halo(0, sta, 0, SIDES, 1)
+    near_copies = field_halo(2, vel, 1, SIDES, 2)
 
     row = lambda shape: lax.broadcasted_iota(jnp.int32, shape, 0)
     lane = lambda shape: lax.broadcasted_iota(jnp.int32, shape, 1)
@@ -120,16 +119,12 @@
     lanes = cy * cz
     n_rows = 6 * cx * ny
     m_shape = (nz, lanes)
-    gather_z = (row(m_shape) // 4 == lax.rem(lane(m_shape), cz)).astype(jnp.float32)
+    gather_z = (row(m_shape) // 4 == lax.rem(lane(m_shape), cz)).astype(jnp.float32).astype(jnp.bfloat16)
     t_shape = (lanes, nz)
     spread_z = (lax.rem(row(t_shape), cz) == lane(t_shape) // 4).astype(jnp.float32)
     k_shape = (n_rows, lanes)
     keep = lax.rem(row(k_shape), ny) // 4 == lane(k_shape) // cz
-    r_shape = (cx * 8, n_rows)
-    src_c, src_x = lane(r_shape) // (cx * ny), lax.rem(lane(r_shape) // ny, cx)
-    gather_y = jnp.where(
-        jnp.logical_and(row(r_shape) // 8 == src_x, lax.rem(row(r_shape), 8) == src_c), 1.0 / 64.0, 0.0
-    )
+    own_y = row((ny, lanes)) // 4 == lane((ny, lanes)) // cz
     p_shape = (n_rows, cx * 8)
     dst_c, dst_x = row(p_shape) // (cx * ny), lax.rem(row(p_shape) // ny, cx)
     spread_y = jnp.where(
@@ -142,6 +137,44 @@
             return carry
 
         lax.fori_loop(0, planes // step, run, 0, unroll=True)
+
+    def restrict(read, first):
+        x_sums = jnp.concatenate(
+            [jnp.sum(read(c, pl.ds(4 * b, 4)), axis=0) for c in range(3) for b in range(cx)], axis=0
+        )
+        high = x_sums.astype(jnp.bfloat16)
+        low = (x_sums - high.astype(jnp.float32)).astype(jnp.bfloat16)
+        z_sums = jnp.dot(high, gather_z, preferred_element_type=jnp.float32) + jnp.dot(
+            low, gather_z, preferred_element_type=jnp.float32
+        )
+        for c in range(3):
+            for b in range(cx):
+                at = (c * cx + b) * ny
+                block = jnp.where(own_y, z_sums[at : at + ny], 0.0)
+                CB[1, 1, b, pl.ds(first + c, 1)] = jnp.sum(block, axis=0, keepdims=True) * (1.0 / 64.0)
+
+    def coarse_halo(first, slot):
+        copies = []
+        for i, (dx, dy) in enumerate(DIRS):
+            xs = {0: pl.ds(0, cx), 1: pl.ds(cx - 3, 3), -1: pl.ds(0, 3)}[dx]
+            rows = pl.ds(first, 3)
+            copies.append(
+                mesh_copy(
+                    CB.at[1, 1, xs, rows], CB.at[1 - dx, 1 - dy, xs, rows],
+                    c_send.at[slot, i], c_recv.at[slot, i], dx, dy,
+                )
+            )
+        for c in copies:
+            c.start()
+        return copies
+
+    locals_[3].wait()
+    rr = jnp.zeros((ny, nz), jnp.float32)
+    for c in range(3):
+        for b in range(cx):
+            r = RS[c, pl.ds(4 * b, 4)]
+            rr = rr + jnp.sum(r * r, axis=0)
+    restrict(lambda c, at: RS[c, at], 0)
 
     for c in locals_[:2]:
         c.wait()
@@ -164,12 +197,20 @@
                 G[3 * n + k, at_x] = grads[k]
 
     sweep(W, nx, 2, sources)
-    source_copies = halo(
-        lambda src, dst: (
-            S.at[pl.ds(0, 2), pl.ds(W + src[0].start, src[0].size), src[1]],
-            S.at[(pl.ds(0, 2),) + dst],
-        ),
-        s_send, s_recv, 3, 2,
+    def source_halo(lo, n, slot, dirs, width):
+        return halo(
+            lambda src, dst: (
+                S.at[pl.ds(lo, n), pl.ds(W + src[0].start, src[0].size), src[1]],
+                S.at[(pl.ds(lo, n),) + dst],
+            ),
+            s_send.at[slot], s_recv.at[slot], dirs, width,
+        )
+
+    source_copies = (
+        source_halo(0, 2, 0, CORNERS, 2)
+        + field_halo(2, vel, 4, CORNERS, 1)
+        + source_halo(0, 1, 1, SIDES, 3)
+        + source_halo(1, 1, 2, SIDES, 2)
     )
     far_copies = halo(
         lambda src, dst: (
@@ -178,17 +219,17 @@
             if dst[1].size == 2
             else F.at[(pl.ds(6, 3),) + dst],
         ),
-        h_send.at[2], h_recv.at[2], 2, 0, 2,
-    )
-    direction_copies = field_halo(1, dirn, 3, 1, 0)
-
-    locals_[3].wait()
-    rr = jnp.zeros((ny, nz), jnp.float32)
-    for c in range(3):
-        for b in range(cx):
-            r = RS[c, pl.ds(4 * b, 4)]
-            TR[c, b] = jnp.sum(r, axis=0)
-            rr = rr + jnp.sum(r * r, axis=0)
+        h_send.at[2], h_recv.at[2], SIDES, 2, 2,
+    )
+    far_copies += halo(
+        lambda src, dst: (
+            vel.at[(pl.ds(0, 3),) + src],
+            FC.at[pl.ds(0, 3), int(dst[0].start > W), pl.ds(0, 3), pl.ds(dst[1].start - ny, 3)],
+        ),
+        h_send.at[5], h_recv.at[5], CORNERS, 3,
+    )
+    direction_copies = field_halo(1, dirn, 3, SIDES, 1)
+    residual_coarse_copies = coarse_halo(0, 0)
 
     locals_[2].wait()
     for c in near_copies:
@@ -226,10 +267,13 @@
     sweep(3, ex - 6, 2, forward_two)
     sweep(4, ex - 8, 2, forward_three)
 
-    u_copies = halo(
-        lambda src, dst: (U.at[pl.ds(W + src[0].start, src[0].size), src[1]], U.at[dst]),
-        u_send, u_recv, W, 3,
-    )
+    def u_halo(slot, dirs, width):
+        return halo(
+            lambda src, dst: (U.at[pl.ds(W + src[0].start, src[0].size), src[1]], U.at[dst]),
+            u_send.at[slot], u_recv.at[slot], dirs, width,
+        )
+
+    u_copies = u_halo(0, CORNERS, 3) + u_halo(1, SIDES, W)
     for c in direction_copies:
         c.wait()
 
@@ -252,6 +296,8 @@
     band, beyond = pl.ds(W, nx), pl.ds(ny, 2 * W)
     from_far = jnp.logical_and(tile_row >= 2, tile_row < 2 * W - 2)
     F[pl.ds(6, 3), band, beyond] = jnp.where(from_far, FV[...], F[pl.ds(6, 3), band, beyond])
+    F[pl.ds(6, 3), pl.ds(W - 3, 3), beyond] = FC[:, 0]
+    F[pl.ds(6, 3), pl.ds(W + nx, 3), beyond] = FC[:, 1]
     for c in u_copies:
         c.wait()
 
@@ -294,20 +340,8 @@
     sweep(3, ex - 6, 2, adjoint_first(lambda i: T[2, pl.ds(i, 2)]))
     sweep(4, ex - 8, 2, adjoint_last)
 
-    for c in range(3):
-        for b in range(cx):
-            TR[3 + c, b] = jnp.sum(IMG[c, pl.ds(4 * b, 4)], axis=0)
-    z_sums = jnp.dot(TR[...].reshape(n_rows, nz), gather_z, precision=HI, preferred_element_type=jnp.float32)
-    rhs = jnp.dot(
-        gather_y, jnp.where(keep, z_sums, 0.0), precision=HI, preferred_element_type=jnp.float32
-    )
-    CB[1, 1] = rhs.reshape(cx, 8, lanes)
-
-    c_copies = []
-    for i, (dx, dy) in enumerate(DIRS):
-        c = mesh_copy(CB.at[1, 1], CB.at[1 - dx, 1 - dy], c_send.at[i], c_recv.at[i], dx, dy)
-        c.start()
-        c_copies.append(c)
+    restrict(lambda c, at: IMG[c, at], 3)
+    c_copies = residual_coarse_copies + coarse_halo(3, 1)
 
     rq = jnp.zeros((ny, nz), jnp.float32)
     qq = jnp.zeros((ny, nz), jnp.float32)
@@ -340,10 +374,10 @@
             + z_up + z_down
         )
         approx = 0.2 * mid + WEIGHT * (b_all[turn + 1 : -turn - 1] + 0.1 * around)
-    e = approx[:, :, lanes : 2 * lanes]
+    r8 = row((8, lanes))
+    e = jnp.where(r8[None] < 6, approx[:, :, lanes : 2 * lanes], 0.0)
     b_own = CB[1, 1]
     same = jnp.sum(b_own * e, axis=0)
-    r8 = row((8, lanes))
     cross = jnp.sum(b_own * jnp.where(r8[None] < 3, pltpu.roll(e, 5, 1), pltpu.roll(e, 3, 1)), axis=0)
     pick = lambda v, lo, hi: flat(jnp.where(jnp.logical_and(r8 >= lo, r8 < hi), v, 0.0))
     sum_a = 0.25 * rr + 64.0 * pick(same, 0, 3)
@@ -425,22 +459,22 @@
                 scratch_shapes=[
                     pltpu.VMEM((9, ex, ey, nz), f32),
                     pltpu.VMEM((3, nx, 2 * W, nz), f32),
+                    pltpu.VMEM((3, 2, 3, 2 * W, nz), f32),
                     pltpu.VMEM((3, ex, ey, nz), f32),
                     pltpu.VMEM((4, ex, ey, nz), f32),
                     pltpu.VMEM((ex, ey, nz), f32),
                     pltpu.VMEM((9, nx, ny, nz), f32),
-                    pltpu.VMEM((6, cx, ny, nz), f32),
                     pltpu.VMEM((3, 3, cx, 8, lanes), f32),
                     pltpu.VMEM((px * py, 1, lanes), f32),
                     dma((6,)),
-                    dma((4, 8)),
-                    dma((4, 8)),
-                    dma((8,)),
-                    dma((8,)),
-                    dma((8,)),
-                    dma((8,)),
-                    dma((8,)),
-                    dma((8,)),
+                    dma((6, 4)),
+                    dma((6, 4)),
+                    dma((3, 4)),
+                    dma((3, 4)),
+                    dma((2, 4)),
+                    dma((2, 4)),
+                    dma((2, 8)),
+                    dma((2, 8)),
                     dma((px * py,)),
                     dma((px * py,)),
                 ],

time: 38.2 us -> 34.2 us (0.90)
  Pallas kernels: 37.4 us -> 33.4 us
    pallas_call x1, Pallas kernels: 36.2 us -> 32.3 us  [local(): pl.pallas_call(functools.partial(kernel, px, py), out_shape=[shape(veloci...]
where the time goes in v2:
time: 34.2 us; the launch traced here: 34.1 us
  Pallas kernels  33.4 us (98%)
  between operations  0.64 us (2%)
    pallas_call x1, Pallas kernels, local(): pl.pallas_call(functools.partial(kernel, px, py), out_shape=[shape(veloci...  32.3 us
    pallas_call x1, Pallas kernels, local(): pl.pallas_call(finish, out_shape=[shape(velocity.shape, f32)] * 3, in_spe...  1.16 us

profile of v2, /device:TPU:0, one launch (start us, length us, event | category | flops | bytes accessed | tf_op | source)
XLA Modules:
  0.0 34.1 jit_solution(13148256868387578031)
XLA Ops:
  0.6 32.3 %shard_map.76 = (f32[3,16,16,128]{3,2,1,0:T(8,128)S(1)}, f32[6,4,16,128]{3,2,1,0:T(8,128)S(1)}, f32[8,128]{1,0:T(8,128)S(1)}, f32[3,3,16,16,128]{4,3,2,1,0:T(8,128)S(1)}) custom-call(f32[3,16,16,128]{3,2,1,0:T(8,128)} %vel.1, f32[3,16,16,128]{3,2,1,0:T(8,128)} %sta.1, f32[3,16,16,128]{3,2,1,0:T(8,128)} %sol.1, f32[3,16,16,128]{3,2,1,0:T(8,128)} %res.1, ...), custom_call_target="tpu_custom_call" | custom-call | tf_op jit(solution)/shard_map/pallas_call | solution.py:451
  32.9 1.2 %shard_map.77 = (f32[3,16,16,128]{3,2,1,0:T(8,128)}, f32[3,16,16,128]{3,2,1,0:T(8,128)}, f32[3,16,16,128]{3,2,1,0:T(8,128)}) custom-call(f32[8,128]{1,0:T(8,128)S(1)} %get-tuple-element.7.scalars, f32[6,4,16,128]{3,2,1,0:T(8,128)S(1)} %get-tuple-element.8.coarse, f32[3,16,16,128]{3,2,1,0:T(8,128)S(1)} %get-tuple-element.9.image, ...), custom_call_target="tpu_custom_call" | custom-call | tf_op jit(solution)/shard_map/pallas_call | solution.py:486

commit v3 on v2

--- a/solution.py
+++ b/solution.py
@@ -99,38 +99,37 @@
             sy, ly, ty = y_span(dy, width, base)
             src, dst = make((pl.ds(sx, lx), pl.ds(sy, ly)), (pl.ds(tx, lx), pl.ds(ty, ly)))
             copies.append(mesh_copy(src, dst, send.at[i], recv.at[i], dx, dy))
+        return copies
+
+    def launch(copies):
         for c in copies:
             c.start()
         return copies
 
-    def field_halo(g, a, slot, *args):
+    def own(g, src):
+        return F.at[pl.ds(3 * g, 3), pl.ds(W + src[0].start, src[0].size), src[1]]
+
+    def field_halo(g, slot, *args):
         return halo(
-            lambda src, dst: (a.at[(pl.ds(0, 3),) + src], F.at[(pl.ds(3 * g, 3),) + dst]),
+            lambda src, dst: (own(g, src), F.at[(pl.ds(3 * g, 3),) + dst]),
             h_send.at[slot], h_recv.at[slot], *args,
         )
 
-    state_copies = field_halo(0, sta, 0, SIDES, 1)
-    near_copies = field_halo(2, vel, 1, SIDES, 2)
+    locals_[0].wait()
+    state_copies = launch(field_halo(0, 0, SIDES, 1))
+    locals_[2].wait()
+    near_copies = launch(field_halo(2, 1, SIDES, 2))
 
     row = lambda shape: lax.broadcasted_iota(jnp.int32, shape, 0)
     lane = lambda shape: lax.broadcasted_iota(jnp.int32, shape, 1)
     cz = nz // 4
     cx, cy = nx // 4, ny // 4
     lanes = cy * cz
-    n_rows = 6 * cx * ny
     m_shape = (nz, lanes)
     gather_z = (row(m_shape) // 4 == lax.rem(lane(m_shape), cz)).astype(jnp.float32).astype(jnp.bfloat16)
     t_shape = (lanes, nz)
-    spread_z = (lax.rem(row(t_shape), cz) == lane(t_shape) // 4).astype(jnp.float32)
-    k_shape = (n_rows, lanes)
-    keep = lax.rem(row(k_shape), ny) // 4 == lane(k_shape) // cz
+    spread_z = (lax.rem(row(t_shape), cz) == lane(t_shape) // 4).astype(jnp.float32).astype(jnp.bfloat16)
     own_y = row((ny, lanes)) // 4 == lane((ny, lanes)) // cz
-    p_shape = (n_rows, cx * 8)
-    dst_c, dst_x = row(p_shape) // (cx * ny), lax.rem(row(p_shape) // ny, cx)
-    spread_y = jnp.where(
-        jnp.logical_and(lane(p_shape) // 8 == dst_x, lax.rem(lane(p_shape), 8) == dst_c), 1.0, 0.0
-    )
-
     def sweep(start, planes, step, body):
         def run(i, carry):
             body(start + i * step)
@@ -138,15 +137,16 @@
 
         lax.fori_loop(0, planes // step, run, 0, unroll=True)
 
+    def two_terms(v, exact):
+        high = v.astype(jnp.bfloat16)
+        low = (v - high.astype(jnp.float32)).astype(jnp.bfloat16)
+        return sum(jnp.dot(part, exact, preferred_element_type=jnp.float32) for part in (low, high))
+
     def restrict(read, first):
         x_sums = jnp.concatenate(
             [jnp.sum(read(c, pl.ds(4 * b, 4)), axis=0) for c in range(3) for b in range(cx)], axis=0
         )
-        high = x_sums.astype(jnp.bfloat16)
-        low = (x_sums - high.astype(jnp.float32)).astype(jnp.bfloat16)
-        z_sums = jnp.dot(high, gather_z, preferred_element_type=jnp.float32) + jnp.dot(
-            low, gather_z, preferred_element_type=jnp.float32
-        )
+        z_sums = two_terms(x_sums, gather_z)
         for c in range(3):
             for b in range(cx):
                 at = (c * cx + b) * ny
@@ -155,18 +155,15 @@
 
     def coarse_halo(first, slot):
         copies = []
-        for i, (dx, dy) in enumerate(DIRS):
+        for i, (dx, dy) in enumerate(CORNERS + SIDES):
             xs = {0: pl.ds(0, cx), 1: pl.ds(cx - 3, 3), -1: pl.ds(0, 3)}[dx]
             rows = pl.ds(first, 3)
-            copies.append(
-                mesh_copy(
-                    CB.at[1, 1, xs, rows], CB.at[1 - dx, 1 - dy, xs, rows],
-                    c_send.at[slot, i], c_recv.at[slot, i], dx, dy,
-                )
+            c = mesh_copy(
+                CB.at[1, 1, xs, rows], CB.at[1 - dx, 1 - dy, xs, rows],
+                c_send.at[slot, i], c_recv.at[slot, i], dx, dy,
             )
-        for c in copies:
-            c.start()
-        return copies
+            copies.append(c)
+        return launch(copies)
 
     locals_[3].wait()
     rr = jnp.zeros((ny, nz), jnp.float32)
@@ -176,27 +173,31 @@
             rr = rr + jnp.sum(r * r, axis=0)
     restrict(lambda c, at: RS[c, at], 0)
 
-    for c in locals_[:2]:
-        c.wait()
+    locals_[1].wait()
     for c in state_copies:
         c.wait()
 
-    def sources(x):
-        own = pl.ds(x, 2)
-        at_x = pl.ds(x - W, 2)
-        d = [F[3 + k, own, pl.ds(0, ny)] for k in range(3)]
-        for n in range(3):
-            f = F[n, own]
-            grads = (
-                (F[n, pl.ds(x + 1, 2)] - F[n, pl.ds(x - 1, 2)])[:, :ny],
-                (up(f, 1) - down(f, 1))[:, :ny],
-                (up(f, 2) - down(f, 2))[:, :ny],
-            )
-            S[n, own, pl.ds(0, ny)] = 0.5 * (d[0] * grads[0] + d[1] * grads[1] + d[2] * grads[2])
-            for k in range(3):
-                G[3 * n + k, at_x] = grads[k]
-
-    sweep(W, nx, 2, sources)
+    def gradient(n, x):
+        f = F[n, pl.ds(x, 2)]
+        return (
+            (F[n, pl.ds(x + 1, 2)] - F[n, pl.ds(x - 1, 2)])[:, :ny],
+            (up(f, 1) - down(f, 1))[:, :ny],
+            (up(f, 2) - down(f, 2))[:, :ny],
+        )
+
+    def sources(moments):
+        def body(x):
+            own = pl.ds(x, 2)
+            d = [F[3 + k, own, pl.ds(0, ny)] for k in range(3)]
+            for n in moments:
+                grads = gradient(n, x)
+                S[n, own, pl.ds(0, ny)] = 0.5 * (d[0] * grads[0] + d[1] * grads[1] + d[2] * grads[2])
+                for k in range(3):
+                    G[3 * n + k, pl.ds(x - W, 2)] = grads[k]
+
+        return body
+
+    sweep(W, nx, 2, sources((0, 1)))
     def source_halo(lo, n, slot, dirs, width):
         return halo(
             lambda src, dst: (
@@ -206,15 +207,15 @@
             s_send.at[slot], s_recv.at[slot], dirs, width,
         )
 
-    source_copies = (
+    source_copies = launch(
         source_halo(0, 2, 0, CORNERS, 2)
-        + field_halo(2, vel, 4, CORNERS, 1)
+        + field_halo(2, 4, CORNERS, 1)
         + source_halo(0, 1, 1, SIDES, 3)
         + source_halo(1, 1, 2, SIDES, 2)
     )
     far_copies = halo(
         lambda src, dst: (
-            vel.at[(pl.ds(0, 3),) + src],
+            own(2, src),
             FV.at[pl.ds(0, 3), pl.ds(0, nx), pl.ds(dst[1].start - ny, 2)]
             if dst[1].size == 2
             else F.at[(pl.ds(6, 3),) + dst],
@@ -223,15 +224,16 @@
     )
     far_copies += halo(
         lambda src, dst: (
-            vel.at[(pl.ds(0, 3),) + src],
+            own(2, src),
             FC.at[pl.ds(0, 3), int(dst[0].start > W), pl.ds(0, 3), pl.ds(dst[1].start - ny, 3)],
         ),
         h_send.at[5], h_recv.at[5], CORNERS, 3,
     )
-    direction_copies = field_halo(1, dirn, 3, SIDES, 1)
+    far_copies = launch(far_copies)
+    direction_copies = launch(field_halo(1, 3, SIDES, 1))
     residual_coarse_copies = coarse_halo(0, 0)
-
-    locals_[2].wait()
+    sweep(W, nx, 2, sources((2,)))
+
     for c in near_copies:
         c.wait()
     for c in source_copies:
@@ -273,7 +275,7 @@
             u_send.at[slot], u_recv.at[slot], dirs, width,
         )
 
-    u_copies = u_halo(0, CORNERS, 3) + u_halo(1, SIDES, W)
+    u_copies = launch(u_halo(0, CORNERS, 3) + u_halo(1, SIDES, W))
     for c in direction_copies:
         c.wait()
 
@@ -389,20 +391,35 @@
         l1 == 0, whole(sum_a), jnp.where(l1 == 1, whole(sum_b), jnp.where(l1 == 2, whole(sum_c), whole(dq)))
     )
 
+    around_x = [lax.rem(me_x + i, px) for i in range(px)]
+    around_y = [lax.rem(me_y + j, py) for j in range(py)]
+
     def sums_copy(d):
-        other = peer(d)
+        other = (around_x[d // py], around_y[d % py]) if isinstance(d, int) else peer(d)
         return pltpu.make_async_remote_copy(
             src_ref=AR.at[0], dst_ref=AR.at[d], send_sem=a_send.at[d], recv_sem=a_recv.at[d],
             device_id=other, device_id_type=pl.DeviceIdType.MESH,
         )
 
-    each_peer(lambda d: sums_copy(d).start())
-
-    spread = jnp.dot(spread_y, e.reshape(cx * 8, lanes), precision=HI, preferred_element_type=jnp.float32)
-    fine = jnp.dot(jnp.where(keep, spread, 0.0), spread_z, precision=HI, preferred_element_type=jnp.float32)
-    PR[...] = fine.reshape(6, cx, ny, nz)
-
-    each_peer(lambda d: sums_copy(d).wait())
+    if total <= 64:
+        far_y = sorted(range(py), key=lambda j: -abs(2 * j - py) if j else 1)
+        far_x = sorted(range(px), key=lambda i: abs(2 * i - px))
+        order = [i * py + j for j in far_y for i in far_x if i or j]
+        for d in order:
+            sums_copy(d).start()
+    else:
+        each_peer(lambda d: sums_copy(d).start())
+
+    wide = jnp.concatenate(
+        [jnp.where(own_y, e[b, c : c + 1], 0.0) for c in range(6) for b in range(cx)], axis=0
+    )
+    PR[...] = two_terms(wide, spread_z).reshape(6, cx, ny, nz)
+
+    if total <= 64:
+        for d in range(1, total):
+            sums_copy(d).wait()
+    else:
+        each_peer(lambda d: sums_copy(d).wait())
     sums = jnp.sum(AR[...], axis=0)
     rz, mixed, square, curvature = (
         jnp.sum(jnp.where(l1 == i, sums, 0.0), axis=1, keepdims=True) for i in range(4)

time: 34.2 us -> 33.7 us (0.985)
  Pallas kernels: 33.4 us -> 32.9 us
    pallas_call x1, Pallas kernels: 32.3 us -> 31.7 us  [local(): pl.pallas_call(functools.partial(kernel, px, py), out_shape=[shape(veloci...]
where the time goes in v3:
time: 33.7 us; the launch traced here: 33.5 us
  Pallas kernels  32.9 us (98%)
  between operations  0.64 us (2%)
    pallas_call x1, Pallas kernels, local(): pl.pallas_call(functools.partial(kernel, px, py), out_shape=[shape(veloci...  31.7 us
    pallas_call x1, Pallas kernels, local(): pl.pallas_call(finish, out_shape=[shape(velocity.shape, f32)] * 3, in_spe...  1.16 us

profile of v3, /device:TPU:0, one launch (start us, length us, event | category | flops | bytes accessed | tf_op | source)
XLA Modules:
  0.0 33.5 jit_solution(14230493810647006861)
XLA Ops:
  0.6 31.7 %shard_map.76 = (f32[3,16,16,128]{3,2,1,0:T(8,128)S(1)}, f32[6,4,16,128]{3,2,1,0:T(8,128)S(1)}, f32[8,128]{1,0:T(8,128)S(1)}, f32[3,3,16,16,128]{4,3,2,1,0:T(8,128)S(1)}) custom-call(f32[3,16,16,128]{3,2,1,0:T(8,128)} %vel.1, f32[3,16,16,128]{3,2,1,0:T(8,128)} %sta.1, f32[3,16,16,128]{3,2,1,0:T(8,128)} %sol.1, f32[3,16,16,128]{3,2,1,0:T(8,128)} %res.1, ...), custom_call_target="tpu_custom_call" | custom-call | tf_op jit(solution)/shard_map/pallas_call | solution.py:468
  32.4 1.2 %shard_map.77 = (f32[3,16,16,128]{3,2,1,0:T(8,128)}, f32[3,16,16,128]{3,2,1,0:T(8,128)}, f32[3,16,16,128]{3,2,1,0:T(8,128)}) custom-call(f32[8,128]{1,0:T(8,128)S(1)} %get-tuple-element.7.scalars, f32[6,4,16,128]{3,2,1,0:T(8,128)S(1)} %get-tuple-element.8.coarse, f32[3,16,16,128]{3,2,1,0:T(8,128)S(1)} %get-tuple-element.9.image, ...), custom_call_target="tpu_custom_call" | custom-call | tf_op jit(solution)/shard_map/pallas_call | solution.py:503

commit v4 on v3

--- a/solution.py
+++ b/solution.py
@@ -385,10 +385,15 @@
     sum_a = 0.25 * rr + 64.0 * pick(same, 0, 3)
     sum_b = 0.5 * rq + 64.0 * pick(cross, 0, 6)
     sum_c = 0.25 * qq + 64.0 * pick(same, 3, 6)
-    whole = lambda v: jnp.broadcast_to(jnp.sum(v, axis=1, keepdims=True), (1, lanes))
-    l1 = lane((1, lanes))
+    def folded(v):
+        v = v + pltpu.roll(v, lanes // 2, 1)
+        return v + pltpu.roll(v, lanes // 4, 1)
+
+    quarter = lane((1, lanes)) // (lanes // 4)
     AR[0] = jnp.where(
-        l1 == 0, whole(sum_a), jnp.where(l1 == 1, whole(sum_b), jnp.where(l1 == 2, whole(sum_c), whole(dq)))
+        quarter < 2,
+        jnp.where(quarter == 0, folded(sum_a), folded(sum_b)),
+        jnp.where(quarter == 2, folded(sum_c), folded(dq)),
     )
 
     around_x = [lax.rem(me_x + i, px) for i in range(px)]
@@ -422,7 +427,7 @@
         each_peer(lambda d: sums_copy(d).wait())
     sums = jnp.sum(AR[...], axis=0)
     rz, mixed, square, curvature = (
-        jnp.sum(jnp.where(l1 == i, sums, 0.0), axis=1, keepdims=True) for i in range(4)
+        jnp.sum(jnp.where(quarter == i, sums, 0.0), axis=1, keepdims=True) for i in range(4)
     )
     alpha = rz / curvature
     beta = (rz - alpha * mixed + alpha * alpha * square) / rz

time: 33.7 us -> 33.8 us (level)
  no operation moved by 1% of the time
where the time goes in v4:
time: 33.8 us; the launch traced here: 33.6 us
  Pallas kernels  33 us (98%)
  between operations  0.64 us (2%)
    pallas_call x1, Pallas kernels, local(): pl.pallas_call(functools.partial(kernel, px, py), out_shape=[shape(veloci...  31.8 us
    pallas_call x1, Pallas kernels, local(): pl.pallas_call(finish, out_shape=[shape(velocity.shape, f32)] * 3, in_spe...  1.16 us

profile of v4, /device:TPU:0, one launch (start us, length us, event | category | flops | bytes accessed | tf_op | source)
XLA Modules:
  0.0 33.6 jit_solution(2577815528310281509)
XLA Ops:
  0.6 31.8 %shard_map.76 = (f32[3,16,16,128]{3,2,1,0:T(8,128)S(1)}, f32[6,4,16,128]{3,2,1,0:T(8,128)S(1)}, f32[8,128]{1,0:T(8,128)S(1)}, f32[3,3,16,16,128]{4,3,2,1,0:T(8,128)S(1)}) custom-call(f32[3,16,16,128]{3,2,1,0:T(8,128)} %vel.1, f32[3,16,16,128]{3,2,1,0:T(8,128)} %sta.1, f32[3,16,16,128]{3,2,1,0:T(8,128)} %sol.1, f32[3,16,16,128]{3,2,1,0:T(8,128)} %res.1, ...), custom_call_target="tpu_custom_call" | custom-call | tf_op jit(solution)/shard_map/pallas_call | solution.py:473
  32.4 1.2 %shard_map.77 = (f32[3,16,16,128]{3,2,1,0:T(8,128)}, f32[3,16,16,128]{3,2,1,0:T(8,128)}, f32[3,16,16,128]{3,2,1,0:T(8,128)}) custom-call(f32[8,128]{1,0:T(8,128)S(1)} %get-tuple-element.7.scalars, f32[6,4,16,128]{3,2,1,0:T(8,128)S(1)} %get-tuple-element.8.coarse, f32[3,16,16,128]{3,2,1,0:T(8,128)S(1)} %get-tuple-element.9.image, ...), custom_call_target="tpu_custom_call" | custom-call | tf_op jit(solution)/shard_map/pallas_call | solution.py:508
